TPU v7x, 256 devices: a whole 4x4x8 slice. The times are simulated.
256 devices in a mesh: sx: 8 (over z), sy: 32 (over y, x, core).
Axes of the slice: x: 4, y: 4, z: 8, core: 2. Of those that a mesh axis runs over, the one named last changes fastest.
Arguments:
- loads: float32 [12288, 4096], P('sx', 'sy'), may hold values from -6 to 6
- dual_op: bfloat16 [12288, 49152], P('sx', 'sy'), as said below
- dirichlet: bfloat16 [12288, 49152], P('sx', 'sy'), as said below
- corner_coupling: bfloat16 [128, 49152], P('sx', 'sy'), may hold values from -0.625 to 0.625
- corner_map: int32 [8, 512], P('sx', 'sy'), may hold values from 0 to 2047, as said below
- coarse_inverse: float32 [2048, 2048], P('sy'), as said below
Outputs:
- multipliers: float32 [12288, 4096], P('sx', 'sy')
- residual: float32 [12288, 4096], P('sx', 'sy')
Inputs may be any that keep to these rules, and one draw needn't show every extreme that they name: `corner_map`: every coarse unknown is named by exactly two entries over all subdomains. `dual_op`: each subdomain's block is symmetric positive definite. `dirichlet`: each subdomain's block is symmetric positive definite. `coarse_inverse`: symmetric positive definite.
All inputs are finite; a program needn't handle non-finite values.
Results may differ from a plain program's by a relative error of at most 0.014.
Values sent between devices are 32-bit elements; how exact they have to be, the bound alone decides.
No kernel may reach another device: no remote copies, remote signals or barrier semaphores. Data moves between devices by JAX's collectives and lax.ppermute only.
A program may use at most 64 MiB of HBM per device.

v0:
```python
import jax
import jax.numpy as jnp
from jax import lax
from jax.sharding import PartitionSpec as P

FACE = 320
EDGE = 64
ITERS = 4
HALF = 0.5
HIGH = lax.Precision.HIGHEST


def passed_along(value, axis, steps):
    count = lax.axis_size(axis)
    first, last = (max(0, -steps), min(count, count - steps))
    return lax.ppermute(value, axis, [(source, source + steps) for source in range(first, last)])


def padded(block, sides, width):
    for axis, dim in sides:
        count = lax.axis_size(axis)
        forward = [(i, i + 1) for i in range(count - 1)]
        backward = [(target, source) for source, target in forward]
        low = lax.ppermute(
            lax.slice_in_dim(block, block.shape[dim] - width, None, axis=dim), axis, forward
        )
        high = lax.ppermute(lax.slice_in_dim(block, 0, width, axis=dim), axis, backward)
        block = jnp.concatenate([low, block, high], axis=dim)
    return block


def split_blocks(field):
    widths = [FACE, FACE, FACE, FACE, EDGE, EDGE, EDGE, EDGE]
    pieces = []
    start = 0
    for width in widths:
        pieces.append(field[start : start + width])
        start = start + width
    return pieces


def assemble(field):
    pieces = split_blocks(field)
    upper_face = passed_along(pieces[1], "sx", 1)
    lower_face = passed_along(pieces[0], "sx", -1)
    left_face = passed_along(pieces[3], "sy", 1)
    right_face = passed_along(pieces[2], "sy", -1)
    stacked = jnp.concatenate([pieces[4], pieces[5], pieces[6], pieces[7]], axis=0)[None, None]
    bordered = padded(stacked, (("sx", 0), ("sy", 1)), 1)
    incoming = [
        upper_face,
        lower_face,
        left_face,
        right_face,
        bordered[0, 0, 3 * EDGE : 4 * EDGE],
        bordered[0, 2, 2 * EDGE : 3 * EDGE],
        bordered[2, 0, EDGE : 2 * EDGE],
        bordered[2, 2, 0:EDGE],
    ]
    return jnp.concatenate([mine + HALF * theirs for mine, theirs in zip(pieces, incoming)], axis=0)


def operate(direction, dual_op, corner_coupling, selector, coarse_inverse):
    spread = assemble(direction)
    rounded = spread.astype(jnp.bfloat16)
    local = jnp.dot(dual_op, rounded, preferred_element_type=jnp.float32)
    corner_part = jnp.dot(corner_coupling, rounded, preferred_element_type=jnp.float32)
    scattered = jnp.dot(selector.T, corner_part, precision=HIGH)
    coarse_sum = lax.psum(scattered, ("sx", "sy"))
    owned_rows = jnp.dot(coarse_inverse, coarse_sum, precision=HIGH)
    solution = lax.all_gather(owned_rows, "sy", axis=0, tiled=True)
    picked = jnp.dot(selector, solution, precision=HIGH)
    correction = jnp.dot(corner_coupling.astype(jnp.float32).T, picked, precision=HIGH)
    return assemble(local + correction)


def residual_norm(residual, smoothed):
    return lax.psum(jnp.sum(residual * smoothed, axis=0), ("sx", "sy"))


def body(loads, dual_op, dirichlet, corner_coupling, corner_map, coarse_inverse):
    corners = corner_map.shape[1]
    coarse_order = coarse_inverse.shape[1]
    selector = (
        corner_map[0][:, None] == lax.broadcasted_iota(jnp.int32, (corners, coarse_order), 1)
    ).astype(jnp.float32)

    def smooth(residual):
        return jnp.dot(dirichlet, residual.astype(jnp.bfloat16), preferred_element_type=jnp.float32)

    multipliers = jnp.zeros_like(loads)
    residual = loads
    smoothed = smooth(residual)
    direction = smoothed
    current = residual_norm(residual, smoothed)
    for step in range(ITERS):
        image = operate(direction, dual_op, corner_coupling, selector, coarse_inverse)
        alpha = current / lax.psum(jnp.sum(direction * image, axis=0), ("sx", "sy"))
        multipliers = multipliers + alpha * direction
        residual = residual - alpha * image
        if step + 1 < ITERS:
            smoothed = smooth(residual)
            following = residual_norm(residual, smoothed)
            direction = smoothed + following / current * direction
            current = following
    return (multipliers, residual)


def solution(mesh):
    in_specs = (
        P("sx", "sy"),
        P("sx", "sy"),
        P("sx", "sy"),
        P("sx", "sy"),
        P("sx", "sy"),
        P("sy", None),
    )
    out_specs = (P("sx", "sy"), P("sx", "sy"))
    return jax.shard_map(body, mesh=mesh, in_specs=in_specs, out_specs=out_specs, check_vma=False)
```

profile of v0, /device:TPU:1, one launch (start us, length us, event | category | flops | bytes accessed | tf_op | source)
XLA Modules:
  0.0 2106.7 jit_solution(1776008902199709787)
XLA Ops:
  7.2 4.0 fusion.7
  12.6 5.0 collective-permute-start.4
  22.5 4.3 collective-permute-start.2
  37.2 4.4 collective-permute-done.7
  43.7 265.5 %all-reduce.6.cloned.1.call-done = f32[2048,128]{1,0:T(8,128)} async-done(((f32[2048,128]{1,0:T(8,128)}), f32[2048,128]{1,0:T(8,128)}) %all-reduce.6.cloned.1.call-update) | async-done | bytes 1048592 | tf_op jit(solution)/shard_map/psum | solution.py:69
  311.9 3.7 fusion.122
  315.6 45.0 %all-gather.5.cloned.1.call-done = f32[2048,128]{1,0:T(8,128)} async-done(((f32[64,128]{1,0:T(8,128)}), f32[2048,128]{1,0:T(8,128)}) %all-gather.5.cloned.1.call-update) | async-done | bytes 1048592 | tf_op jit(solution)/shard_map/all_gather | solution.py:71
  367.4 4.0 collective-permute-start.12
  373.4 4.5 collective-permute-start.14
  379.7 3.6 collective-permute-start.10
  385.7 4.4 collective-permute-done.11
  391.3 82.7 %all-reduce = (f32[128]{0:T(128)S(1)}, f32[128]{0:T(128)S(1)}) all-reduce(f32[128]{0:T(128)S(1)} %get-tuple-element.3, f32[128]{0:T(128)S(1)} %get-tuple-element.2), channel_id=1, replica_groups=mesh['sx'=8,'sy'=32] {'sx','sy'}, use_global_device_ids=true, to_apply=%region_1.0 | all-reduce | flops 256 | bytes 2048 | tf_op jit(solution)/shard_map/psum | solution.py:78
  475.3 4.6 multiply_reduce_fusion.5
  479.9 74.7 %psum.87 = f32[128]{0:T(128)S(1)} all-reduce(f32[128]{0:T(128)S(1)} %get-tuple-element.40), channel_id=1, replica_groups=mesh['sx'=8,'sy'=32] {'sx','sy'}, use_global_device_ids=true, to_apply=%region_6.0 | all-reduce | flops 128 | bytes 1024 | tf_op jit(solution)/shard_map/psum | solution.py:78
  557.1 4.0 collective-permute-start.20
  564.4 4.1 collective-permute-start.18
  578.8 4.4 collective-permute-done.23
  585.6 263.1 %all-reduce.8.cloned.1.call-done = f32[2048,128]{1,0:T(8,128)} async-done(((f32[2048,128]{1,0:T(8,128)}), f32[2048,128]{1,0:T(8,128)}) %all-reduce.8.cloned.1.call-update) | async-done | bytes 1048592 | tf_op jit(solution)/shard_map/psum | solution.py:69
  851.3 4.6 fusion.123
  856.0 44.0 %all-gather.7.cloned.1.call-done = f32[2048,128]{1,0:T(8,128)} async-done(((f32[64,128]{1,0:T(8,128)}), f32[2048,128]{1,0:T(8,128)}) %all-gather.7.cloned.1.call-update) | async-done | bytes 1048592 | tf_op jit(solution)/shard_map/all_gather | solution.py:71
  907.8 4.0 collective-permute-start.28
  913.8 4.5 collective-permute-start.30
  926.1 4.4 collective-permute-done.27
  931.7 82.7 %psum.89 = f32[128]{0:T(128)S(1)} all-reduce(f32[128]{0:T(128)S(1)} %multiply_reduce_fusion.4), channel_id=1, replica_groups=mesh['sx'=8,'sy'=32] {'sx','sy'}, use_global_device_ids=true, to_apply=%region_9.0 | all-reduce | flops 128 | bytes 1024 | tf_op jit(solution)/shard_map/psum | solution.py:98
  1016.5 4.6 multiply_reduce_fusion.3
  1021.2 74.7 %psum.90 = f32[128]{0:T(128)S(1)} all-reduce(f32[128]{0:T(128)S(1)} %get-tuple-element.42), channel_id=1, replica_groups=mesh['sx'=8,'sy'=32] {'sx','sy'}, use_global_device_ids=true, to_apply=%region_11.0 | all-reduce | flops 128 | bytes 1024 | tf_op jit(solution)/shard_map/psum | solution.py:78
  1098.4 4.0 collective-permute-start.36
  1105.7 4.1 collective-permute-start.34
  1120.1 4.4 collective-permute-done.39
  1126.6 263.3 %all-reduce.10.cloned.1.call-done = f32[2048,128]{1,0:T(8,128)} async-done(((f32[2048,128]{1,0:T(8,128)}), f32[2048,128]{1,0:T(8,128)}) %all-reduce.10.cloned.1.call-update) | async-done | bytes 1048592 | tf_op jit(solution)/shard_map/psum | solution.py:69
  1392.6 4.6 fusion.124
  1397.2 43.7 %all-gather.9.cloned.1.call-done = f32[2048,128]{1,0:T(8,128)} async-done(((f32[64,128]{1,0:T(8,128)}), f32[2048,128]{1,0:T(8,128)}) %all-gather.9.cloned.1.call-update) | async-done | bytes 1048592 | tf_op jit(solution)/shard_map/all_gather | solution.py:71
  1448.9 4.0 collective-permute-start.44
  1454.8 4.5 collective-permute-start.46
  1467.1 4.4 collective-permute-done.43
  1472.7 82.7 %psum.92 = f32[128]{0:T(128)S(1)} all-reduce(f32[128]{0:T(128)S(1)} %multiply_reduce_fusion.2), channel_id=1, replica_groups=mesh['sx'=8,'sy'=32] {'sx','sy'}, use_global_device_ids=true, to_apply=%region_14.0 | all-reduce | flops 128 | bytes 1024 | tf_op jit(solution)/shard_map/psum | solution.py:98
  1557.8 4.6 multiply_reduce_fusion.1
  1562.4 74.8 %psum.93 = f32[128]{0:T(128)S(1)} all-reduce(f32[128]{0:T(128)S(1)} %get-tuple-element.44), channel_id=1, replica_groups=mesh['sx'=8,'sy'=32] {'sx','sy'}, use_global_device_ids=true, to_apply=%region_16.0 | all-reduce | flops 128 | bytes 1024 | tf_op jit(solution)/shard_map/psum | solution.py:78
  1639.8 4.0 collective-permute-start.52
  1647.1 3.9 collective-permute-start.50
  1661.4 4.4 collective-permute-done.55
  1667.9 263.3 %all-reduce.12.cloned.1.call-done = f32[2048,128]{1,0:T(8,128)} async-done(((f32[2048,128]{1,0:T(8,128)}), f32[2048,128]{1,0:T(8,128)}) %all-reduce.12.cloned.1.call-update) | async-done | bytes 1048592 | tf_op jit(solution)/shard_map/psum | solution.py:69
  1933.9 4.6 fusion.125
  1938.5 43.8 %all-gather.11.cloned.1.call-done = f32[2048,128]{1,0:T(8,128)} async-done(((f32[64,128]{1,0:T(8,128)}), f32[2048,128]{1,0:T(8,128)}) %all-gather.11.cloned.1.call-update) | async-done | bytes 1048592 | tf_op jit(solution)/shard_map/all_gather | solution.py:71
  1990.3 4.0 collective-permute-start.60
  1996.2 4.5 collective-permute-start.62
  2008.5 4.4 collective-permute-done.59
  2014.1 82.7 %psum.95 = f32[128]{0:T(128)S(1)} all-reduce(f32[128]{0:T(128)S(1)} %multiply_reduce_fusion), channel_id=1, replica_groups=mesh['sx'=8,'sy'=32] {'sx','sy'}, use_global_device_ids=true, to_apply=%region_19.0 | all-reduce | flops 128 | bytes 1024 | tf_op jit(solution)/shard_map/psum | solution.py:98
  (269 shorter events, 163.1 us)
Async XLA Ops:
  7.2 302.0 %all-reduce.6.cloned.1.call-start = ((), (), s32[]{:S(2)}) async-start(), calls=%async_computation | async-start | bytes 2097152 | tf_op jit(solution)/shard_map/psum | solution.py:69
  11.3 15.6 collective-permute-start.5
  12.6 16.2 collective-permute-start.4
  17.6 14.8 collective-permute-start
  21.2 13.3 collective-permute-start.1
  22.5 12.0 collective-permute-start.2
  32.5 9.1 collective-permute-start.7
  43.7 316.9 %all-gather.5.cloned.1.call-start = ((), (), s32[]{:S(2)}) async-start(), calls=%async_computation.1 | async-start | bytes 1081344 | tf_op jit(solution)/shard_map/all_gather | solution.py:71
  311.8 536.8 %all-reduce.8.cloned.1.call-start = ((), (), s32[]{:S(2)}) async-start(), calls=%async_computation.2 | async-start | bytes 2097152 | tf_op jit(solution)/shard_map/psum | solution.py:69
  362.9 8.5 collective-permute-start.8
  371.5 13.9 collective-permute-start.9
  373.4 16.7 collective-permute-start.14
  377.8 12.3 collective-permute-start.15
  555.8 12.7 collective-permute-start.21
  557.1 13.3 collective-permute-start.20
  561.2 13.0 collective-permute-start.16
  563.1 13.0 collective-permute-start.17
  564.4 11.7 collective-permute-start.18
  574.1 9.1 collective-permute-start.23
  585.3 314.6 %all-gather.7.cloned.1.call-start = ((), (), s32[]{:S(2)}) async-start(), calls=%async_computation.3 | async-start | bytes 1081344 | tf_op jit(solution)/shard_map/all_gather | solution.py:71
  851.3 538.6 %all-reduce.10.cloned.1.call-start = ((), (), s32[]{:S(2)}) async-start(), calls=%async_computation.4 | async-start | bytes 2097152 | tf_op jit(solution)/shard_map/psum | solution.py:69
  903.3 8.5 collective-permute-start.24
  911.9 13.9 collective-permute-start.25
  913.8 16.7 collective-permute-start.30
  918.3 12.3 collective-permute-start.31
  1097.1 12.7 collective-permute-start.37
  1098.4 13.3 collective-permute-start.36
  1102.4 13.0 collective-permute-start.32
  1104.4 13.0 collective-permute-start.33
  1105.7 11.7 collective-permute-start.34
  1115.4 9.1 collective-permute-start.39
  1126.6 314.4 %all-gather.9.cloned.1.call-start = ((), (), s32[]{:S(2)}) async-start(), calls=%async_computation.5 | async-start | bytes 1081344 | tf_op jit(solution)/shard_map/all_gather | solution.py:71
  1392.6 538.7 %all-reduce.12.cloned.1.call-start = ((), (), s32[]{:S(2)}) async-start(), calls=%async_computation.6 | async-start | bytes 2097152 | tf_op jit(solution)/shard_map/psum | solution.py:69
  1444.4 8.5 collective-permute-start.40
  1452.9 14.1 collective-permute-start.41
  1454.8 16.7 collective-permute-start.46
  1459.3 12.3 collective-permute-start.47
  1638.5 12.5 collective-permute-start.53
  1639.8 13.2 collective-permute-start.52
  1643.8 12.8 collective-permute-start.48
  1645.8 12.9 collective-permute-start.49
  1647.1 11.6 collective-permute-start.50
  1656.7 9.1 collective-permute-start.55
  1667.9 314.4 %all-gather.11.cloned.1.call-start = ((), (), s32[]{:S(2)}) async-start(), calls=%async_computation.7 | async-start | bytes 1081344 | tf_op jit(solution)/shard_map/all_gather | solution.py:71
  1985.8 8.5 collective-permute-start.56
  1994.3 13.9 collective-permute-start.57
  1996.2 16.7 collective-permute-start.62
  2000.7 12.3 collective-permute-start.63
  (36 other events, 675.6 us)
Sparse Core Ops, SparseCore 0:
  43.8 265.3 all-reduce.5
  312.3 48.2 all-gather.4
  585.4 263.1 all-reduce.7
  851.6 48.2 all-gather.6
  1126.7 263.1 all-reduce.9
  1392.7 48.2 all-gather.8
  1668.0 263.2 all-reduce.11
  1934.0 48.2 all-gather.10
where the time goes:
time: 2110 us
  waiting for transfers between devices  1280 us (61%)
  blocking collectives  555 us (26%)
  starting transfers between devices  171 us (8%)
  matrix products  66.4 us (3%)
    psum x4, waiting for transfers between devices, operate(): coarse_sum = lax.psum(scattered, ('sx', 'sy'))  1060 us
    psum x4, blocking collectives, residual_norm(): return lax.psum(jnp.sum(residual * smoothed, axis=0), ('sx', 'sy'))  307 us
    psum x3, blocking collectives, body(): alpha = current / lax.psum(jnp.sum(direction * image, axis=0), ('sx', 'sy'))  248 us
    all_gather x4, waiting for transfers between devices, operate(): solution = lax.all_gather(owned_rows, 'sy', axis=0, tiled=True)  176 us
    ppermute x32, starting transfers between devices, passed_along(): lax.ppermute(value, axis, [(source, source + steps) for source in range(f...  79 us
    ppermute x16, starting transfers between devices, padded(): lax.ppermute(lax.slice_in_dim(block, block.shape[dim] - width, None, axis...  65.3 us
  transfers between devices with their start and end apart: 72, of which 28 were waited for; matrix products, arithmetic and copies ran while one was open for 1% of the time, Pallas kernels for 0%

commit v1 on v0

--- a/solution.py
+++ b/solution.py
@@ -2,6 +2,7 @@
 import jax.numpy as jnp
 from jax import lax
 from jax.sharding import PartitionSpec as P
+from jax.lax import psum
 
 FACE = 320
 EDGE = 64
@@ -95,7 +96,7 @@
     current = residual_norm(residual, smoothed)
     for step in range(ITERS):
         image = operate(direction, dual_op, corner_coupling, selector, coarse_inverse)
-        alpha = current / lax.psum(jnp.sum(direction * image, axis=0), ("sx", "sy"))
+        alpha = current / psum(psum(jnp.sum(direction * image, axis=0), axis_name="sx"), "sy")
         multipliers = multipliers + alpha * direction
         residual = residual - alpha * image
         if step + 1 < ITERS:

time: 2110 us -> 2170 us (1.028)
  blocking collectives: 555 us -> 617 us
    psum x3 -> x8, blocking collectives: 248 us -> 313 us  [the longest x4 254 us: body(): psum(psum(jnp.sum(direction * image, axis=0), axis_name='sx'), 'sy')]
where the time goes in v1:
time: 2170 us; the launch traced here: 2160 us
  waiting for transfers between devices  1280 us (59%)
  blocking collectives  617 us (28%)
  starting transfers between devices  170 us (8%)
  matrix products  66.4 us (3%)
    psum x4, waiting for transfers between devices, operate(): coarse_sum = lax.psum(scattered, ('sx', 'sy'))  1050 us
    psum x4, blocking collectives, residual_norm(): return lax.psum(jnp.sum(residual * smoothed, axis=0), ('sx', 'sy'))  304 us
    psum x4, blocking collectives, body(): psum(psum(jnp.sum(direction * image, axis=0), axis_name='sx'), 'sy')  254 us
    all_gather x4, waiting for transfers between devices, operate(): solution = lax.all_gather(owned_rows, 'sy', axis=0, tiled=True)  176 us
    ppermute x32, starting transfers between devices, passed_along(): lax.ppermute(value, axis, [(source, source + steps) for source in range(f...  77.7 us
    ppermute x16, starting transfers between devices, padded(): lax.ppermute(lax.slice_in_dim(block, block.shape[dim] - width, None, axis...  65.6 us
    psum x4, blocking collectives, body(): psum(jnp.sum(direction * image, axis=0), axis_name='sx')  58.6 us
  transfers between devices with their start and end apart: 72, of which 28 were waited for; matrix products, arithmetic and copies ran while one was open for 1% of the time, Pallas kernels for 0%

profile of v1, /device:TPU:1, one launch (start us, length us, event | category | flops | bytes accessed | tf_op | source)
XLA Modules:
  0.0 2164.9 jit_solution(225033356254219687)
XLA Ops:
  7.2 4.0 fusion.7
  12.6 5.0 collective-permute-start.4
  22.5 4.3 collective-permute-start.2
  37.2 4.4 collective-permute-done.7
  43.7 265.5 %all-reduce.5.cloned.1.call-done = f32[2048,128]{1,0:T(8,128)} async-done(((f32[2048,128]{1,0:T(8,128)}), f32[2048,128]{1,0:T(8,128)}) %all-reduce.5.cloned.1.call-update) | async-done | bytes 1048592 | tf_op jit(solution)/shard_map/psum | solution.py:70
  315.6 45.0 %all-gather.5.cloned.1.call-done = f32[2048,128]{1,0:T(8,128)} async-done(((f32[64,128]{1,0:T(8,128)}), f32[2048,128]{1,0:T(8,128)}) %all-gather.5.cloned.1.call-update) | async-done | bytes 1048592 | tf_op jit(solution)/shard_map/all_gather | solution.py:72
  367.4 4.0 collective-permute-start.12
  373.4 4.5 collective-permute-start.14
  385.7 4.4 collective-permute-done.11
  391.3 82.7 %psum.112 = f32[128]{0:T(128)S(1)} all-reduce(f32[128]{0:T(128)S(1)} %get-tuple-element.3), channel_id=1, replica_groups=mesh['sx'=8,'sy'=32] {'sx','sy'}, use_global_device_ids=true, to_apply=%region_1.0 | all-reduce | flops 128 | bytes 1024 | tf_op jit(solution)/shard_map/psum | solution.py:79
  474.1 13.6 psum.114
  487.7 66.4 %psum.115 = f32[128]{0:T(128)S(1)} all-reduce(f32[128]{0:T(128)S(1)} %psum.114), channel_id=1, replica_groups=mesh['sx'=8,'sy'=32] {'sy'}, use_global_device_ids=true, to_apply=%region_5.0 | all-reduce | flops 128 | bytes 1024 | tf_op jit(solution)/shard_map/psum | solution.py:99
  555.4 4.6 multiply_reduce_fusion.5
  560.0 72.6 %psum.116 = f32[128]{0:T(128)S(1)} all-reduce(f32[128]{0:T(128)S(1)} %get-tuple-element.38), channel_id=1, replica_groups=mesh['sx'=8,'sy'=32] {'sx','sy'}, use_global_device_ids=true, to_apply=%region_7.0 | all-reduce | flops 128 | bytes 1024 | tf_op jit(solution)/shard_map/psum | solution.py:79
  635.1 4.3 collective-permute-start.20
  657.6 4.4 collective-permute-done.23
  664.1 261.5 %all-reduce.7.cloned.1.call-done = f32[2048,128]{1,0:T(8,128)} async-done(((f32[2048,128]{1,0:T(8,128)}), f32[2048,128]{1,0:T(8,128)}) %all-reduce.7.cloned.1.call-update) | async-done | bytes 1048592 | tf_op jit(solution)/shard_map/psum | solution.py:70
  928.3 4.6 fusion.123
  932.9 44.0 %all-gather.7.cloned.1.call-done = f32[2048,128]{1,0:T(8,128)} async-done(((f32[64,128]{1,0:T(8,128)}), f32[2048,128]{1,0:T(8,128)}) %all-gather.7.cloned.1.call-update) | async-done | bytes 1048592 | tf_op jit(solution)/shard_map/all_gather | solution.py:72
  984.8 4.0 collective-permute-start.28
  990.8 4.5 collective-permute-start.30
  1003.1 4.4 collective-permute-done.27
  1008.6 15.0 psum.118
  1023.6 62.5 %psum.119 = f32[128]{0:T(128)S(1)} all-reduce(f32[128]{0:T(128)S(1)} %psum.118), channel_id=1, replica_groups=mesh['sx'=8,'sy'=32] {'sy'}, use_global_device_ids=true, to_apply=%region_11.0 | all-reduce | flops 128 | bytes 1024 | tf_op jit(solution)/shard_map/psum | solution.py:99
  1088.3 4.6 multiply_reduce_fusion.3
  1092.9 74.3 %psum.120 = f32[128]{0:T(128)S(1)} all-reduce(f32[128]{0:T(128)S(1)} %get-tuple-element.40), channel_id=1, replica_groups=mesh['sx'=8,'sy'=32] {'sx','sy'}, use_global_device_ids=true, to_apply=%region_13.0 | all-reduce | flops 128 | bytes 1024 | tf_op jit(solution)/shard_map/psum | solution.py:79
  1169.8 4.0 collective-permute-start.36
  1190.6 4.4 collective-permute-done.39
  1197.1 263.0 %all-reduce.9.cloned.1.call-done = f32[2048,128]{1,0:T(8,128)} async-done(((f32[2048,128]{1,0:T(8,128)}), f32[2048,128]{1,0:T(8,128)}) %all-reduce.9.cloned.1.call-update) | async-done | bytes 1048592 | tf_op jit(solution)/shard_map/psum | solution.py:70
  1462.8 4.6 fusion.124
  1467.4 43.7 %all-gather.9.cloned.1.call-done = f32[2048,128]{1,0:T(8,128)} async-done(((f32[64,128]{1,0:T(8,128)}), f32[2048,128]{1,0:T(8,128)}) %all-gather.9.cloned.1.call-update) | async-done | bytes 1048592 | tf_op jit(solution)/shard_map/all_gather | solution.py:72
  1519.1 4.0 collective-permute-start.44
  1525.0 4.5 collective-permute-start.46
  1537.3 4.4 collective-permute-done.43
  1542.9 15.0 psum.122
  1557.9 62.5 %psum.123 = f32[128]{0:T(128)S(1)} all-reduce(f32[128]{0:T(128)S(1)} %psum.122), channel_id=1, replica_groups=mesh['sx'=8,'sy'=32] {'sy'}, use_global_device_ids=true, to_apply=%region_17.0 | all-reduce | flops 128 | bytes 1024 | tf_op jit(solution)/shard_map/psum | solution.py:99
  1622.8 4.6 multiply_reduce_fusion.1
  1627.4 74.3 %psum.124 = f32[128]{0:T(128)S(1)} all-reduce(f32[128]{0:T(128)S(1)} %get-tuple-element.42), channel_id=1, replica_groups=mesh['sx'=8,'sy'=32] {'sx','sy'}, use_global_device_ids=true, to_apply=%region_19.0 | all-reduce | flops 128 | bytes 1024 | tf_op jit(solution)/shard_map/psum | solution.py:79
  1704.3 4.0 collective-permute-start.52
  1725.1 4.4 collective-permute-done.55
  1731.6 263.0 %all-reduce.11.cloned.1.call-done = f32[2048,128]{1,0:T(8,128)} async-done(((f32[2048,128]{1,0:T(8,128)}), f32[2048,128]{1,0:T(8,128)}) %all-reduce.11.cloned.1.call-update) | async-done | bytes 1048592 | tf_op jit(solution)/shard_map/psum | solution.py:70
  1997.3 4.6 fusion.125
  2001.9 43.8 %all-gather.11.cloned.1.call-done = f32[2048,128]{1,0:T(8,128)} async-done(((f32[64,128]{1,0:T(8,128)}), f32[2048,128]{1,0:T(8,128)}) %all-gather.11.cloned.1.call-update) | async-done | bytes 1048592 | tf_op jit(solution)/shard_map/all_gather | solution.py:72
  2053.7 4.0 collective-permute-start.60
  2059.6 4.5 collective-permute-start.62
  2071.9 4.4 collective-permute-done.59
  2077.5 15.0 psum.126
  2092.5 62.5 %psum.127 = f32[128]{0:T(128)S(1)} all-reduce(f32[128]{0:T(128)S(1)} %psum.126), channel_id=1, replica_groups=mesh['sx'=8,'sy'=32] {'sy'}, use_global_device_ids=true, to_apply=%region_23.0 | all-reduce | flops 128 | bytes 1024 | tf_op jit(solution)/shard_map/psum | solution.py:99
  (274 shorter events, 181.0 us)
Async XLA Ops:
  7.2 302.0 %all-reduce.5.cloned.1.call-start = ((), (), s32[]{:S(2)}) async-start(), calls=%async_computation | async-start | bytes 2097152 | tf_op jit(solution)/shard_map/psum | solution.py:70
  11.3 15.6 collective-permute-start.5
  12.6 16.2 collective-permute-start.4
  17.6 14.8 collective-permute-start
  21.2 13.3 collective-permute-start.1
  22.5 12.0 collective-permute-start.2
  32.5 9.1 collective-permute-start.7
  43.7 316.9 %all-gather.5.cloned.1.call-start = ((), (), s32[]{:S(2)}) async-start(), calls=%async_computation.1 | async-start | bytes 1081344 | tf_op jit(solution)/shard_map/all_gather | solution.py:72
  311.8 613.8 %all-reduce.7.cloned.1.call-start = ((), (), s32[]{:S(2)}) async-start(), calls=%async_computation.2 | async-start | bytes 2097152 | tf_op jit(solution)/shard_map/psum | solution.py:70
  362.9 8.5 collective-permute-start.8
  371.5 13.9 collective-permute-start.9
  373.4 16.7 collective-permute-start.14
  377.8 12.3 collective-permute-start.15
  633.8 13.4 collective-permute-start.21
  635.1 14.1 collective-permute-start.20
  639.5 13.4 collective-permute-start.16
  642.8 12.2 collective-permute-start.17
  644.1 10.9 collective-permute-start.18
  652.9 9.1 collective-permute-start.23
  664.1 312.8 %all-gather.7.cloned.1.call-start = ((), (), s32[]{:S(2)}) async-start(), calls=%async_computation.3 | async-start | bytes 1081344 | tf_op jit(solution)/shard_map/all_gather | solution.py:72
  928.2 531.9 %all-reduce.9.cloned.1.call-start = ((), (), s32[]{:S(2)}) async-start(), calls=%async_computation.4 | async-start | bytes 2097152 | tf_op jit(solution)/shard_map/psum | solution.py:70
  980.3 8.5 collective-permute-start.24
  988.9 13.9 collective-permute-start.25
  990.8 16.7 collective-permute-start.30
  995.2 12.3 collective-permute-start.31
  1168.5 11.7 collective-permute-start.37
  1169.8 12.4 collective-permute-start.36
  1173.8 12.0 collective-permute-start.32
  1175.8 12.0 collective-permute-start.33
  1177.1 10.7 collective-permute-start.34
  1185.8 9.1 collective-permute-start.39
  1197.0 314.1 %all-gather.9.cloned.1.call-start = ((), (), s32[]{:S(2)}) async-start(), calls=%async_computation.5 | async-start | bytes 1081344 | tf_op jit(solution)/shard_map/all_gather | solution.py:72
  1462.7 531.9 %all-reduce.11.cloned.1.call-start = ((), (), s32[]{:S(2)}) async-start(), calls=%async_computation.6 | async-start | bytes 2097152 | tf_op jit(solution)/shard_map/psum | solution.py:70
  1514.6 8.5 collective-permute-start.40
  1523.1 13.9 collective-permute-start.41
  1525.0 16.7 collective-permute-start.46
  1529.5 12.3 collective-permute-start.47
  1703.0 11.7 collective-permute-start.53
  1704.3 12.4 collective-permute-start.52
  1708.4 12.0 collective-permute-start.48
  1710.3 12.0 collective-permute-start.49
  1711.6 10.8 collective-permute-start.50
  1720.4 9.1 collective-permute-start.55
  1731.6 314.1 %all-gather.11.cloned.1.call-start = ((), (), s32[]{:S(2)}) async-start(), calls=%async_computation.7 | async-start | bytes 1081344 | tf_op jit(solution)/shard_map/all_gather | solution.py:72
  2049.1 8.5 collective-permute-start.56
  2057.7 13.9 collective-permute-start.57
  2059.6 16.7 collective-permute-start.62
  2064.1 12.3 collective-permute-start.63
  (36 other events, 675.1 us)
Sparse Core Ops, SparseCore 0:
  43.8 265.3 all-reduce.4
  312.3 48.2 all-gather.4
  664.2 261.3 all-reduce.6
  928.6 48.2 all-gather.6
  1197.2 262.9 all-reduce.8
  1462.9 48.2 all-gather.8
  1731.7 262.8 all-reduce.10
  1997.4 48.2 all-gather.10
